TPU v7x, 256 devices: a whole 4x4x8 slice. The times are simulated.
256 devices in a mesh: wide: 128 (over y, z, x), cols: 2 (over core).
Axes of the slice: x: 4, y: 4, z: 8, core: 2. Of those that a mesh axis runs over, the one named last changes fastest.
Arguments:
- factor: float32 [262144, 256], P('wide', 'cols')
- gates: float32 [8, 128, 128], replicated, may hold values from -0.5 to 0.5
- gate_layout: int32 [2048], P('wide'), may hold values from 0 to 7
- jump_masks: int32 [3], replicated, may hold values from 1 to 127
- jump_rates: float32 [3], replicated, may hold values from 0.1 to 0.4
- sketch_perm: int32 [1024], replicated, may hold values from 0 to 1023, each once
- bases: float32 [8, 64, 64], replicated, may hold values from -0.75 to 0.75
- basis_index: int32 [128, 32], P('wide'), may hold values from 0 to 7
Outputs:
- new_factor: float32 [262144, 256], P('wide', 'cols')
- weights: float32 [128, 2048], P('wide', 'cols')
Inputs may be any that keep to these rules, and one draw needn't show every extreme that they name: `jump_masks`: nonzero bit masks over the high qubits. `sketch_perm`: each value appears once.
All inputs are finite; a program needn't handle non-finite values.
Results may differ from a plain program's by a relative error of at most 0.0003.
Values sent between devices are 32-bit elements; how exact they have to be, the bound alone decides.
No kernel may reach another device: no remote copies, remote signals or barrier semaphores. Data moves between devices by JAX's collectives and lax.ppermute only.
A program may use at most 64 MiB of HBM per device.

v0:
```python
import jax
import jax.numpy as jnp
from jax import lax
from jax.sharding import PartitionSpec as P

NS_ITERS = 7
HIGH = lax.Precision.HIGHEST


def apply_blocks(mats, index, data):
    chosen = jnp.take(mats, index, axis=0)
    return jnp.einsum("bij,bjc->bic", chosen, data, precision=HIGH)


def flip_rows(data, mask, count):
    shaped = data.reshape(count, data.shape[0] // count, data.shape[1])
    source = jnp.bitwise_xor(jnp.arange(count, dtype=jnp.int32), mask)
    return jnp.take(shaped, source, axis=0).reshape(data.shape)


def sketch_table(sketch_perm, rank):
    target = sketch_perm % rank
    sign = 1.0 - 2.0 * (sketch_perm // rank % 2).astype(jnp.float32)
    hit = target[:, None] == jnp.arange(rank, dtype=jnp.int32)[None, :]
    return jnp.where(hit, sign[:, None], jnp.zeros((), jnp.float32))


def mixed_stack(source, table, first, coefs, masks, count):
    rank = table.shape[1]
    width = source.shape[1]
    sources = []
    blocks = []
    for k in range(len(coefs)):
        flipped = source if k == 0 else flip_rows(source, masks[k - 1], count)
        sources.append(coefs[k] * flipped)
        blocks.append(lax.dynamic_slice_in_dim(table, k * rank + first, width, 0))
    joined = jnp.concatenate(sources, axis=1)
    table_rows = jnp.concatenate(blocks, axis=0)
    return jnp.dot(joined, table_rows, precision=HIGH, preferred_element_type=jnp.float32)


def newton_root(mat, eye, iters):
    fro = jnp.sqrt(jnp.sum(mat * mat))
    approx = mat / (fro + 1e-06)
    inverse = eye
    for step in range(iters):
        middle = 1.5 * eye - 0.5 * jnp.dot(inverse, approx, precision=HIGH)
        approx = jnp.dot(approx, middle, precision=HIGH)
        inverse = jnp.dot(middle, inverse, precision=HIGH)
    return (approx, inverse, fro)


def per_device(factor, gates, gate_layout, jump_masks, jump_rates, sketch_perm, bases, basis_index):
    rows, width = factor.shape
    order = gates.shape[1]
    count = lax.axis_size("wide")
    halves = lax.axis_size("cols")
    column_index = lax.axis_index("cols")
    rank = width * halves
    jumps = jump_rates.shape[0]
    gated = apply_blocks(gates, gate_layout, factor.reshape(rows // order, order, width)).reshape(
        rows, width
    )
    moved = lax.all_to_all(gated, "wide", split_axis=0, concat_axis=0, tiled=True)
    keep = 1.0 - 0.5 * jnp.sum(jump_rates)
    coefs = [keep] + [jnp.sqrt(jump_rates[k]) for k in range(jumps)]
    table = sketch_table(sketch_perm, rank)
    first = column_index * width
    terms = mixed_stack(moved, table, first, coefs, jump_masks, count)
    sketch_own = lax.psum_scatter(terms, "cols", scatter_dimension=1, tiled=True)
    sketch = lax.all_gather(sketch_own, "cols", axis=1, tiled=True)
    share = rows // halves
    mine = lax.dynamic_slice_in_dim(sketch, column_index * share, share, 0)
    gram_part = lax.dot_general(
        mine, mine, (((0,), (0,)), ((), ())), precision=HIGH, preferred_element_type=jnp.float32
    )
    gram = lax.psum(gram_part, ("wide", "cols"))
    eye = jnp.eye(rank, dtype=jnp.float32)
    unused, inverse, fro = newton_root(gram, eye, NS_ITERS)
    parts = []
    for k in range(jumps + 1):
        right = moved if k == 0 else flip_rows(moved, jump_masks[k - 1], count)
        parts.append(
            coefs[k]
            * lax.dot_general(
                sketch,
                right,
                (((0,), (0,)), ((), ())),
                precision=HIGH,
                preferred_element_type=jnp.float32,
            )
        )
    proj_own = jnp.concatenate(parts, axis=1)
    proj_sum = lax.psum(proj_own, "wide")
    coeff = lax.dot_general(
        inverse,
        proj_sum,
        (((0,), (0,)), ((), ())),
        precision=HIGH,
        preferred_element_type=jnp.float32,
    )
    core_part = lax.dot_general(
        coeff, coeff, (((1,), (1,)), ((), ())), precision=HIGH, preferred_element_type=jnp.float32
    )
    core = lax.psum(core_part, "cols")
    approx_two, unused_two, fro_two = newton_root(core, eye, NS_ITERS)
    root_own = jnp.sqrt(fro_two + 1e-06) * lax.dynamic_slice_in_dim(approx_two, first, width, 1)
    mixing_own = jnp.dot(inverse, root_own, precision=HIGH)
    new_own = jnp.dot(sketch, mixing_own, precision=HIGH)
    rot = bases.shape[1]
    rotated = apply_blocks(bases, basis_index.reshape(-1), new_own.reshape(rows // rot, rot, width))
    partial_value = (jnp.sum(rotated * rotated, axis=2) / rank).reshape(1, rows)
    weights = lax.psum_scatter(partial_value, "cols", scatter_dimension=1, tiled=True)
    return (new_own, weights)


def solution(mesh):
    return jax.shard_map(
        per_device,
        mesh=mesh,
        in_specs=(P("wide", "cols"), P(), P("wide"), P(), P(), P(), P(), P("wide", None)),
        out_specs=(P("wide", "cols"), P("wide", "cols")),
        check_vma=False,
    )
```

profile of v0, /device:TPU:1, one launch (start us, length us, event | category | flops | bytes accessed | tf_op | source)
XLA Modules:
  0.0 657.7 jit_solution(18310592391966807667)
XLA Ops:
  7.2 0.7 compare_select_fusion.5
  8.6 1.7 gather_fusion
  10.3 2.2 fusion.12
  12.5 16.3 %all-to-all-start = ((f32[128,16,128]{2,1,0:T(8,128)}), f32[128,16,128]{2,1,0:T(8,128)S(1)}, u32[]{:S(2)}, u32[]{:S(2)}) async-start(f32[128,16,128]{2,1,0:T(8,128)} %bitcast.1), calls=%async_computation | async-start | bytes 2097152 | tf_op jit(solution)/shard_map/all_to_all | solution.py:64
  34.3 1.2 compare_and_fusion.2
  35.5 1.3 compare_select_fusion
  36.7 1.8 compare_and_fusion
  39.6 16.5 %all-to-all-done = f32[128,16,128]{2,1,0:T(8,128)S(1)} async-done(((f32[128,16,128]{2,1,0:T(8,128)}), f32[128,16,128]{2,1,0:T(8,128)S(1)}, u32[]{:S(2)}, u32[]{:S(2)}) %all-to-all-start) | async-done | bytes 1048608 | tf_op jit(solution)/shard_map/all_to_all | solution.py:64
  56.1 0.8 gather_fusion.3
  56.8 0.9 broadcast_select_fusion.1
  57.7 1.0 copy-done.4
  58.7 1.0 broadcast_multiply_fusion.1
  59.7 0.8 gather_fusion.4
  60.7 1.0 copy-done.5
  61.7 1.0 broadcast_multiply_fusion
  62.7 0.8 gather_fusion.2
  63.9 0.8 copy-done.7
  65.7 4.9 fusion
  70.6 13.1 %reduce-scatter.5.cloned.1.call-done = f32[2048,128]{1,0:T(8,128)} async-done(((f32[2048,256]{1,0:T(8,128)}), f32[2048,128]{1,0:T(8,128)}) %reduce-scatter.5.cloned.1.call-update) | async-done | bytes 1048592 | tf_op jit(solution)/shard_map/reduce_scatter | solution.py:70
  83.8 19.0 %all-gather.2.cloned.1.call-done = f32[2048,256]{1,0:T(8,128)} async-done(((f32[2048,128]{1,0:T(8,128)}), f32[2048,256]{1,0:T(8,128)}) %all-gather.2.cloned.1.call-update) | async-done | bytes 2097168 | tf_op jit(solution)/shard_map/all_gather | solution.py:71
  102.7 4.1 fusion.10
  107.4 5.4 convolution_multiply_fusion.16
  112.8 3.4 convolution_multiply_fusion.15
  116.3 3.4 convolution_multiply_fusion.17
  119.7 3.6 convolution_multiply_fusion.18
  123.3 0.8 pad_maximum_fusion
  124.2 234.4 %all-reduce.4.cloned.1.call-done = f32[256,256]{1,0:T(8,128)} async-done(((f32[256,256]{1,0:T(8,128)}), f32[256,256]{1,0:T(8,128)}) %all-reduce.4.cloned.1.call-update) | async-done | bytes 262160 | tf_op jit(solution)/shard_map/psum | solution.py:77
  358.6 1.6 multiply_reduce_fusion.1
  360.9 1.3 select_subtract_fusion.13
  362.5 1.3 fusion.31
  370.0 1.1 fusion.58
  371.1 206.0 %all-reduce.6.cloned.1.call-done = f32[256,512]{1,0:T(8,128)} async-done(((f32[256,512]{1,0:T(8,128)}), f32[256,512]{1,0:T(8,128)}) %all-reduce.6.cloned.1.call-update) | async-done | bytes 524304 | tf_op jit(solution)/shard_map/psum | solution.py:94
  577.2 1.7 fusion.59
  578.9 1.3 fusion.60
  580.6 1.6 gather_fusion.1
  582.2 30.0 %all-reduce.8.cloned.1.call-done = f32[256,256]{1,0:T(8,128)} async-done(((f32[256,256]{1,0:T(8,128)}), f32[256,256]{1,0:T(8,128)}) %all-reduce.8.cloned.1.call-update) | async-done | bytes 262160 | tf_op jit(solution)/shard_map/psum | solution.py:105
  612.2 1.6 multiply_reduce_fusion
  614.5 1.3 select_subtract_fusion.6
  616.0 1.3 fusion.32
  622.4 1.1 fusion.70
  623.9 1.3 select_subtract_fusion
  625.7 1.4 fusion.28
  627.1 1.8 fusion.72
  629.0 1.0 copy-done.9
  629.9 1.5 fusion.8
  631.5 2.0 div.43
  633.5 15.3 %reduce-scatter.7.cloned.1.call-done = f32[1024,1]{1,0:T(8,128)} async-done(((f32[2048,1]{1,0:T(8,128)}), f32[1024,1]{1,0:T(8,128)}) %reduce-scatter.7.cloned.1.call-update) | async-done | bytes 4112
  648.8 1.8 copy.11
  (101 shorter events, 19.3 us)
Async XLA Ops:
  7.2 3.1 copy-start
  10.3 18.6 %copy-start.16 = (f32[3]{0:T(128)S(1)}, f32[3]{0:T(128)}, u32[]{:S(2)}) copy-start(f32[3]{0:T(128)} %param.14) | copy-start | bytes 40
  10.3 22.6 %copy-start.17 = (s32[3]{0:T(128)S(1)}, s32[3]{0:T(128)}, u32[]{:S(2)}) copy-start(s32[3]{0:T(128)} %param.13) | copy-start | bytes 40
  10.3 28.2 %copy-start.15 = (s32[1024]{0:T(1024)S(1)}, s32[1024]{0:T(1024)}, u32[]{:S(2)}) copy-start(s32[1024]{0:T(1024)} %param.15) | copy-start | bytes 12292
  12.5 43.6 %all-to-all-start = ((f32[128,16,128]{2,1,0:T(8,128)}), f32[128,16,128]{2,1,0:T(8,128)S(1)}, u32[]{:S(2)}, u32[]{:S(2)}) async-start(f32[128,16,128]{2,1,0:T(8,128)} %bitcast.1), calls=%async_computation | async-start | bytes 2097152 | tf_op jit(solution)/shard_map/all_to_all | solution.py:64
  28.8 54.8 %reduce-scatter.5.cloned.1.call-start = ((), (), s32[]{:S(2)}) async-start(), calls=%async_computation.3 | async-start | bytes 3145728 | tf_op jit(solution)/shard_map/reduce_scatter | solution.py:70
  56.1 7.7 %copy-start.2 = (f32[128,16,128]{2,1,0:T(8,128)}, f32[128,16,128]{2,1,0:T(8,128)S(1)}, u32[]{:S(2)}) copy-start(f32[128,16,128]{2,1,0:T(8,128)S(1)} %all-to-all-done) | copy-start | bytes 3145732
  57.7 1.0 copy-start.4
  60.7 1.0 copy-start.5
  61.7 1.8 copy-start.18
  63.7 1.0 copy-start.7
  63.7 1.6 copy-start.12
  63.8 1.9 copy-start.13
  63.8 1.9 copy-start.14
  70.5 13.2 %copy-start.19 = (s32[1,32]{1,0:T(1,128)S(1)}, s32[1,32]{1,0:T(1,128)}, u32[]{:S(2)}) copy-start(s32[1,32]{1,0:T(1,128)} %param.17) | copy-start | bytes 388
  70.6 32.2 %all-gather.2.cloned.1.call-start = ((), (), s32[]{:S(2)}) async-start(), calls=%async_computation.4 | async-start | bytes 3145728 | tf_op jit(solution)/shard_map/all_gather | solution.py:71
  83.7 274.9 %all-reduce.4.cloned.1.call-start = ((), (), s32[]{:S(2)}) async-start(), calls=%async_computation.5 | async-start | bytes 524288 | tf_op jit(solution)/shard_map/psum | solution.py:77
  106.9 5.9 copy-start.1
  106.9 470.3 %all-reduce.6.cloned.1.call-start = ((), (), s32[]{:S(2)}) async-start(), calls=%async_computation.6 | async-start | bytes 1048576 | tf_op jit(solution)/shard_map/psum | solution.py:94
  107.4 5.4 copy-start.6
  112.8 3.5 copy-start.8
  116.3 3.5 copy-start.3
  124.2 488.0 %all-reduce.8.cloned.1.call-start = ((), (), s32[]{:S(2)}) async-start(), calls=%async_computation.7 | async-start | bytes 524288 | tf_op jit(solution)/shard_map/psum | solution.py:105
  369.6 210.9 %copy-start.11 = (f32[8,64,64]{2,1,0:T(8,128)S(1)}, f32[8,64,64]{2,1,0:T(8,128)}, u32[]{:S(2)}) copy-start(f32[8,64,64]{2,1,0:T(8,128)} %param.16) | copy-start | bytes 393220
  580.3 68.5 %reduce-scatter.7.cloned.1.call-start = ((), (), s32[]{:S(2)}) async-start(), calls=%async_computation.8 | async-start | bytes 1572864
  625.7 4.3 copy-start.10
  629.0 1.0 copy-start.9
Sparse Core Ops, SparseCore 0:
  70.7 12.9 reduce-scatter.4
  85.6 17.0 all-gather.1
  109.1 249.4 all-reduce.3
  365.3 211.7 all-reduce.5
  580.4 31.7 all-reduce.7
  633.6 15.1 reduce-scatter.6
where the time goes:
time: 666 us; the launch traced here: 658 us
  waiting for transfers between devices  534 us (80%)
  matrix products  55.9 us (8%)
  between operations  19.3 us (3%)
  starting transfers between devices  17.3 us (3%)
  local copies, waits for them, and re-layouts  16.1 us (2%)
  other arithmetic  14.9 us (2%)
    psum x1, waiting for transfers between devices, per_device(): gram = lax.psum(gram_part, ('wide', 'cols'))  234 us
    psum x1, waiting for transfers between devices, per_device(): proj_sum = lax.psum(proj_own, 'wide')  206 us
    psum x1, waiting for transfers between devices, per_device(): core = lax.psum(core_part, 'cols')  30 us
    all_gather x1, waiting for transfers between devices, per_device(): sketch = lax.all_gather(sketch_own, 'cols', axis=1, tiled=True)  19 us
    all_to_all x1, waiting for transfers between devices, per_device(): lax.all_to_all(gated, 'wide', split_axis=0, concat_axis=0, tiled=True)  16.5 us
    all_to_all x1, starting transfers between devices, per_device(): lax.all_to_all(gated, 'wide', split_axis=0, concat_axis=0, tiled=True)  16.3 us
    dot_general x4, matrix products, per_device(): lax.dot_general(sketch, right, (((0,), (0,)), ((), ())), precision=HIGH,...  15.9 us
    unnamed x7, waiting for transfers between devices  15.4 us
  transfers between devices with their start and end apart: 7, of which 7 were waited for; matrix products, arithmetic and copies ran while one was open for 6% of the time, Pallas kernels for 0%

commit v1 on v0

--- a/solution.py
+++ b/solution.py
@@ -74,7 +74,7 @@
     gram_part = lax.dot_general(
         mine, mine, (((0,), (0,)), ((), ())), precision=HIGH, preferred_element_type=jnp.float32
     )
-    gram = lax.psum(gram_part, ("wide", "cols"))
+    gram = lax.psum(lax.psum(gram_part, "wide"), "cols")
     eye = jnp.eye(rank, dtype=jnp.float32)
     unused, inverse, fro = newton_root(gram, eye, NS_ITERS)
     parts = []

time: 666 us -> 471 us (0.71)
  waiting for transfers between devices: 534 us -> 342 us
    psum x2, waiting for transfers between devices: 440 us -> 250 us  [per_device(): gram = lax.psum(lax.psum(gram_part, 'wide'), 'cols')]
  transfers between devices with their start and end apart: 7 -> 7, of which waited for: 7 -> 7; matrix products, arithmetic and copies ran while one was open for 6% -> 2% of each run, Pallas kernels for 0% -> 0%
where the time goes in v1:
time: 471 us; the launch traced here: 464 us
  waiting for transfers between devices  342 us (73%)
  matrix products  53.8 us (11%)
  between operations  19.2 us (4%)
  starting transfers between devices  17.3 us (4%)
  local copies, waits for them, and re-layouts  16.8 us (4%)
  other arithmetic  14.8 us (3%)
    psum x2, waiting for transfers between devices, per_device(): gram = lax.psum(lax.psum(gram_part, 'wide'), 'cols')  250 us
    psum x1, waiting for transfers between devices, per_device(): core = lax.psum(core_part, 'cols')  28.6 us
    all_gather x1, waiting for transfers between devices, per_device(): sketch = lax.all_gather(sketch_own, 'cols', axis=1, tiled=True)  18.5 us
    dot_general x4, matrix products, per_device(): lax.dot_general(sketch, right, (((0,), (0,)), ((), ())), precision=HIGH,...  17.2 us
    all_to_all x1, waiting for transfers between devices, per_device(): lax.all_to_all(gated, 'wide', split_axis=0, concat_axis=0, tiled=True)  16.6 us
    all_to_all x1, starting transfers between devices, per_device(): lax.all_to_all(gated, 'wide', split_axis=0, concat_axis=0, tiled=True)  16.3 us
    unnamed x7, waiting for transfers between devices  15.4 us
    reduce_scatter x1, waiting for transfers between devices, per_device(): lax.psum_scatter(terms, 'cols', scatter_dimension=1, tiled=True)  13.1 us
  transfers between devices with their start and end apart: 7, of which 7 were waited for; matrix products, arithmetic and copies ran while one was open for 2% of the time, Pallas kernels for 0%

profile of v1, /device:TPU:1, one launch (start us, length us, event | category | flops | bytes accessed | tf_op | source)
XLA Modules:
  0.0 463.6 jit_solution(2797367765873250057)
XLA Ops:
  7.2 0.7 compare_select_fusion.5
  8.6 1.7 gather_fusion
  10.3 2.2 fusion.12
  12.5 16.3 %all-to-all-start = ((f32[128,16,128]{2,1,0:T(8,128)}), f32[128,16,128]{2,1,0:T(8,128)S(1)}, u32[]{:S(2)}, u32[]{:S(2)}) async-start(f32[128,16,128]{2,1,0:T(8,128)} %bitcast.1), calls=%async_computation | async-start | bytes 2097152 | tf_op jit(solution)/shard_map/all_to_all | solution.py:64
  34.2 1.2 compare_and_fusion.2
  35.3 1.3 compare_select_fusion
  36.6 1.8 compare_and_fusion
  38.8 0.7 constant_dynamic-slice_fusion.3
  39.5 16.6 %all-to-all-done = f32[128,16,128]{2,1,0:T(8,128)S(1)} async-done(((f32[128,16,128]{2,1,0:T(8,128)}), f32[128,16,128]{2,1,0:T(8,128)S(1)}, u32[]{:S(2)}, u32[]{:S(2)}) %all-to-all-start) | async-done | bytes 1048608 | tf_op jit(solution)/shard_map/all_to_all | solution.py:64
  56.1 0.8 gather_fusion.3
  56.8 0.9 broadcast_select_fusion.1
  57.7 1.0 copy-done.3
  58.7 1.1 broadcast_multiply_fusion.1
  59.8 0.8 gather_fusion.4
  60.7 1.0 copy-done.5
  61.7 1.0 broadcast_multiply_fusion
  62.8 0.8 gather_fusion.2
  63.9 0.8 copy-done.7
  65.7 4.9 %fusion = f32[2048,256]{1,0:T(8,128)} fusion(f32[2048,128]{1,0:T(8,128)S(1)} %copy-done.13, f32[2048,128]{1,0:T(8,128)S(1)} %copy-done.12, f32[2048,128]{1,0:T(8,128)S(1)} %get-tuple-element.19, f32[2048,128]{1,0:T(8,128)S(1)} %get-tuple-element.20, f32[128,256]{1,0:T(8,128)S(1)} %get-tuple-element.6, f32[128,256]{1,0:T(8,128)S(1)} %get-tuple-element.7, ...), kind=kOutput, calls=%fused_computation.5 | convolution fusion | flops 3224764416 | bytes 6815744 | tf_op jit(solution)/shard_map/dot_general | solution.py:39
  70.6 13.1 %reduce-scatter.5.cloned.1.call-done = f32[2048,128]{1,0:T(8,128)} async-done(((f32[2048,256]{1,0:T(8,128)}), f32[2048,128]{1,0:T(8,128)}) %reduce-scatter.5.cloned.1.call-update) | async-done | bytes 1048592 | tf_op jit(solution)/shard_map/reduce_scatter | solution.py:70
  84.2 18.5 %all-gather.2.cloned.1.call-done = f32[2048,256]{1,0:T(8,128)} async-done(((f32[2048,128]{1,0:T(8,128)}), f32[2048,256]{1,0:T(8,128)}) %all-gather.2.cloned.1.call-update) | async-done | bytes 2097168 | tf_op jit(solution)/shard_map/all_gather | solution.py:71
  102.7 5.4 %convolution_multiply_fusion.18 = f32[256,128]{1,0:T(8,128)S(1)} fusion(f32[2048,256]{1,0:T(8,128)} %all-gather.2.cloned.1.call-done, f32[2048,128]{1,0:T(8,128)} %bitcast.115, f32[]{:T(128)S(6)} %sub.57), kind=kOutput, calls=%fused_computation.46 | convolution fusion | flops 805339136 | bytes 3276804 | tf_op jit(solution)/shard_map/dot_general | solution.py:85
  108.2 4.7 %convolution_multiply_fusion.17 = f32[256,128]{1,0:T(8,128)S(1)} fusion(f32[2048,256]{1,0:T(8,128)S(1)} %copy-done.1, f32[2048,128]{1,0:T(8,128)} %bitcast.118, f32[]{:T(128)} %bitcast.3), kind=kOutput, calls=%fused_computation.45 | convolution fusion | flops 805339136 | bytes 3276804 | tf_op jit(solution)/shard_map/dot_general | solution.py:85
  112.9 3.4 convolution_multiply_fusion.16
  116.4 3.6 convolution_multiply_fusion.15
  120.0 0.8 pad_maximum_fusion
  120.8 2.5 fusion.10
  123.5 215.6 %all-reduce.9.cloned.1.call-done = (f32[256,256]{1,0:T(8,128)}, f32[256,512]{1,0:T(8,128)}) async-done(((f32[256,256]{1,0:T(8,128)}, f32[256,512]{1,0:T(8,128)}), (f32[256,256]{1,0:T(8,128)}, f32[256,512]{1,0:T(8,128)})) %all-reduce.9.cloned.1.call-update) | async-done | bytes 786448 | tf_op jit(solution)/shard_map/psum | solution.py:77
  339.1 33.9 %all-reduce.5.cloned.1.call-done = f32[256,256]{1,0:T(8,128)} async-done(((f32[256,256]{1,0:T(8,128)}), f32[256,256]{1,0:T(8,128)}) %all-reduce.5.cloned.1.call-update) | async-done | bytes 262160 | tf_op jit(solution)/shard_map/psum | solution.py:77
  373.1 1.6 multiply_reduce_fusion.1
  375.4 1.3 select_subtract_fusion.13
  376.9 1.3 fusion.31
  384.9 0.7 copy-done.11
  386.2 1.3 fusion.60
  387.9 1.6 gather_fusion.1
  389.5 28.6 %all-reduce.7.cloned.1.call-done = f32[256,256]{1,0:T(8,128)} async-done(((f32[256,256]{1,0:T(8,128)}), f32[256,256]{1,0:T(8,128)}) %all-reduce.7.cloned.1.call-update) | async-done | bytes 262160 | tf_op jit(solution)/shard_map/psum | solution.py:105
  418.1 1.6 multiply_reduce_fusion
  420.4 1.3 select_subtract_fusion.6
  421.9 1.3 fusion.32
  428.3 1.1 fusion.70
  429.8 1.3 select_subtract_fusion
  431.6 1.4 fusion.28
  433.0 1.9 fusion.72
  434.9 1.0 copy-done.8
  435.8 1.5 fusion.8
  437.4 2.0 div.43
  439.4 15.3 %reduce-scatter.7.cloned.1.call-done = f32[1024,1]{1,0:T(8,128)} async-done(((f32[2048,1]{1,0:T(8,128)}), f32[1024,1]{1,0:T(8,128)}) %reduce-scatter.7.cloned.1.call-update) | async-done | bytes 4112
  454.7 1.8 copy.11
  (103 shorter events, 19.6 us)
Async XLA Ops:
  7.2 3.1 copy-start
  10.3 18.6 %copy-start.17 = (f32[3]{0:T(128)S(1)}, f32[3]{0:T(128)}, u32[]{:S(2)}) copy-start(f32[3]{0:T(128)} %param.14) | copy-start | bytes 40
  10.3 22.6 %copy-start.18 = (s32[3]{0:T(128)S(1)}, s32[3]{0:T(128)}, u32[]{:S(2)}) copy-start(s32[3]{0:T(128)} %param.13) | copy-start | bytes 40
  10.3 28.1 %copy-start.16 = (s32[1024]{0:T(1024)S(1)}, s32[1024]{0:T(1024)}, u32[]{:S(2)}) copy-start(s32[1024]{0:T(1024)} %param.15) | copy-start | bytes 12292
  12.5 43.6 %all-to-all-start = ((f32[128,16,128]{2,1,0:T(8,128)}), f32[128,16,128]{2,1,0:T(8,128)S(1)}, u32[]{:S(2)}, u32[]{:S(2)}) async-start(f32[128,16,128]{2,1,0:T(8,128)} %bitcast.1), calls=%async_computation | async-start | bytes 2097152 | tf_op jit(solution)/shard_map/all_to_all | solution.py:64
  28.8 54.8 %reduce-scatter.5.cloned.1.call-start = ((), (), s32[]{:S(2)}) async-start(), calls=%async_computation.3 | async-start | bytes 3145728 | tf_op jit(solution)/shard_map/reduce_scatter | solution.py:70
  56.1 7.7 %copy-start.2 = (f32[128,16,128]{2,1,0:T(8,128)}, f32[128,16,128]{2,1,0:T(8,128)S(1)}, u32[]{:S(2)}) copy-start(f32[128,16,128]{2,1,0:T(8,128)S(1)} %all-to-all-done) | copy-start | bytes 3145732
  57.7 1.0 copy-start.3
  60.7 1.0 copy-start.5
  61.7 1.8 copy-start.19
  63.7 1.0 copy-start.7
  63.8 1.6 copy-start.12
  63.8 1.9 copy-start.13
  63.8 1.9 copy-start.15
  70.6 32.2 %all-gather.2.cloned.1.call-start = ((), (), s32[]{:S(2)}) async-start(), calls=%async_computation.4 | async-start | bytes 3145728 | tf_op jit(solution)/shard_map/all_gather | solution.py:71
  83.7 255.3 %all-reduce.9.cloned.1.call-start = ((), (), s32[]{:S(2)}) async-start(), calls=%async_computation.8 | async-start | bytes 1572864 | tf_op jit(solution)/shard_map/psum | solution.py:77
  102.7 5.4 %copy-start.1 = (f32[2048,256]{1,0:T(8,128)S(1)}, f32[2048,256]{1,0:T(8,128)}, u32[]{:S(2)}) copy-start(f32[2048,256]{1,0:T(8,128)} %all-gather.2.cloned.1.call-done) | copy-start | bytes 6291460
  108.2 4.8 %copy-start.4 = (f32[128,16,128]{2,1,0:T(8,128)S(1)}, f32[128,16,128]{2,1,0:T(8,128)}, u32[]{:S(2)}) copy-start(f32[128,16,128]{2,1,0:T(8,128)} %copy-done.3) | copy-start | bytes 3145732
  112.9 3.5 copy-start.6
  120.0 219.1 %copy-start.20 = (s32[1,32]{1,0:T(1,128)S(1)}, s32[1,32]{1,0:T(1,128)}, u32[]{:S(2)}) copy-start(s32[1,32]{1,0:T(1,128)} %param.17) | copy-start | bytes 388
  123.4 249.7 %all-reduce.5.cloned.1.call-start = ((), (), s32[]{:S(2)}) async-start(), calls=%async_computation.5 | async-start | bytes 524288 | tf_op jit(solution)/shard_map/psum | solution.py:77
  339.0 79.0 %all-reduce.7.cloned.1.call-start = ((), (), s32[]{:S(2)}) async-start(), calls=%async_computation.6 | async-start | bytes 524288 | tf_op jit(solution)/shard_map/psum | solution.py:105
  382.9 2.7 copy-start.14
  384.1 3.8 copy-start.10
  384.9 0.7 copy-start.11
  387.6 67.1 %reduce-scatter.7.cloned.1.call-start = ((), (), s32[]{:S(2)}) async-start(), calls=%async_computation.7 | async-start | bytes 1572864
  431.6 4.3 copy-start.9
  434.9 1.0 copy-start.8
Sparse Core Ops, SparseCore 0:
  70.7 12.9 reduce-scatter.4
  85.6 17.0 all-gather.1
  123.5 215.4 all-reduce.8
  341.5 31.5 all-reduce.4
  387.7 30.3 all-reduce.6
  439.5 15.1 reduce-scatter.6
